TPU v7x, 256 devices: a whole 4x4x8 slice. The times are simulated.
256 devices in a mesh: brick: 32 (over z, x), scene: 8 (over y, core).
Axes of the slice: x: 4, y: 4, z: 8, core: 2. Of those that a mesh axis runs over, the one named last changes fastest.
Arguments:
- features: float32 [8, 128, 64, 512], P('scene', 'brick'), may hold values from -6 to 6
- cotangent: float32 [8, 128, 64, 512], P('scene', 'brick'), may hold values from -6 to 6
- first_kernel: float32 [27, 64, 64], replicated, may hold values from -0.15625 to 0.15625
- second_kernel: float32 [27, 64, 64], replicated, may hold values from -0.15625 to 0.15625
- counts: int32 [32], P('brick'), may hold values from 1 to 4, as said below
- neighbours: int32 [128, 26], P('brick'), may hold values from -1 to 127, as said below
Outputs:
- out_features: float32 [8, 128, 64, 512], P('scene', 'brick')
- feature_grad: float32 [8, 128, 64, 512], P('scene', 'brick')
- first_grad: float32 [27, 64, 64], replicated
- second_grad: float32 [27, 64, 64], replicated
Inputs may be any that keep to these rules, and one draw needn't show every extreme that they name: Index d of brick owns counts[d] bricks in its slots 0 to counts[d] - 1; some index owns 4. `neighbours`: entries name occupied slots; the relation is symmetric (if slot t is the neighbour of s in direction (a, b, c), s is the neighbour of t in (-a, -b, -c)); unoccupied slots have only -1. A neighbour in a direction with c = 0 is owned by the same index of brick, with c = 1 by the same or the next index, with c = -1 by the same or the previous index.
All inputs are finite; a program needn't handle non-finite values.
Results may differ from a plain program's by a relative error of at most 0.0057.
Values may be sent and summed in bfloat16 or wider, within the bound.
No kernel may reach another device: no remote copies, remote signals or barrier semaphores. Data moves between devices by JAX's collectives and lax.ppermute only.
A program may use at most 128 MiB of HBM per device.

v0:
```python
import jax
import jax.numpy as jnp
from jax import lax
from jax.sharding import PartitionSpec as P

E = 8
offsets = [(a, b, c) for a in (-1, 0, 1) for b in (-1, 0, 1) for c in (-1, 0, 1)]
directions = [item for item in offsets if item != (0, 0, 0)]


def with_halo(shard, sides, width):
    for axis, dim in sides:
        devices, length = (lax.axis_size(axis), shard.shape[dim])
        up = [(i, (i + 1) % devices) for i in range(devices - 1)]
        down = [(j, i) for i, j in up]
        last = lax.slice_in_dim(shard, length - width, length, axis=dim)
        first = lax.slice_in_dim(shard, 0, width, axis=dim)
        before = lax.ppermute(last, axis, up)
        after = lax.ppermute(first, axis, down)
        shard = jnp.concatenate([before, shard, after], axis=dim)
    return shard


def source_range(offset, edge_cells):
    if offset < 0:
        return (edge_cells - 1, edge_cells)
    if offset == 0:
        return (0, edge_cells)
    return (0, 1)


def assemble(center, sources, indices, present, edge_cells):
    pieces = {}
    pieces[0, 0, 0] = center
    for number, (a, b, c) in enumerate(directions):
        source = sources[c + 1]
        range_i = source_range(a, edge_cells)
        range_j = source_range(b, edge_cells)
        depth_range = source_range(c, edge_cells) if c == 0 else (0, 1)
        slab_part = source[
            :, :, range_i[0] : range_i[1], range_j[0] : range_j[1], depth_range[0] : depth_range[1]
        ]
        last_row = source.shape[0] - 1
        chosen_rows = jnp.clip(indices[c + 1][:, number], 0, last_row).astype(jnp.int32)
        picked = jnp.take(slab_part, chosen_rows, axis=0)
        pieces[a, b, c] = jnp.where(
            present[:, number][:, None, None, None, None], picked, jnp.zeros_like(picked)
        )
    planes = []
    for a in (-1, 0, 1):
        lines = []
        for b in (-1, 0, 1):
            lines.append(jnp.concatenate([pieces[a, b, c] for c in (-1, 0, 1)], axis=4))
        planes.append(jnp.concatenate(lines, axis=3))
    return jnp.concatenate(planes, axis=2)


def columns_of(padded):
    lead_shape = padded.shape[:3]
    stacked = []
    for number in range(27):
        a, b, c = offsets[number]
        part = padded[..., 1 + a : 1 + a + E, 1 + b : 1 + b + E, 1 + c : 1 + c + E]
        stacked.append(part.reshape(lead_shape + (E * E * E,)))
    joined = jnp.stack(stacked, axis=2)
    return joined.reshape((lead_shape[0], lead_shape[1], 27 * lead_shape[2], E * E * E))


def apply_flat(columns, weight_flat):
    return jnp.einsum("ko,nskp->nsop", weight_flat, columns, preferred_element_type=jnp.float32)


def kernel_terms(columns, errors_b):
    total = jnp.einsum("nskp,nsop->ko", columns, errors_b, preferred_element_type=jnp.float32)
    return total.reshape(27, errors_b.shape[2], errors_b.shape[2])


def slope(values):
    sig = jax.nn.sigmoid(values)
    return sig * (1.0 + values * (1.0 - sig))


def body(features, cotangent, first_kernel, second_kernel, counts, neighbours):
    scenes_here, slots_here, channels, voxels = features.shape
    device_row = lax.axis_index("brick")
    occupied = (jnp.arange(slots_here, dtype=jnp.int32) < counts[0]).astype(jnp.float32)[
        None, :, None, None
    ]
    inputs = features * occupied
    upstream = cotangent * occupied
    present = neighbours >= 0
    index_mid = neighbours - device_row * slots_here
    index_low = index_mid + slots_here
    indices = (index_low, index_mid, index_mid)
    first_b = first_kernel.astype(jnp.bfloat16)
    second_b = second_kernel.astype(jnp.bfloat16)
    first_fwd = first_b.reshape(27 * channels, channels)
    second_fwd = second_b.reshape(27 * channels, channels)
    first_back = jnp.transpose(first_b[::-1], (0, 2, 1)).reshape(27 * channels, channels)
    second_back = jnp.transpose(second_b[::-1], (0, 2, 1)).reshape(27 * channels, channels)
    cube_shape = (scenes_here, slots_here, channels, E, E, E)

    def padded_of(values):
        rounded = values.astype(jnp.bfloat16)
        cubes = rounded.reshape(cube_shape)
        extended = with_halo(rounded, (("brick", 1),), slots_here)
        below = extended[:, :slots_here].reshape(cube_shape)[..., E - 1 : E]
        above = extended[:, 2 * slots_here :].reshape(cube_shape)[..., 0:1]
        pool_low = jnp.concatenate([below, cubes[..., E - 1 : E]], axis=1)
        pool_high = jnp.concatenate([cubes[..., 0:1], above], axis=1)

        def build(centre, lower_pool, upper_pool):
            return assemble(centre, (lower_pool, centre, upper_pool), indices, present, E)

        return columns_of(jax.vmap(build)(cubes, pool_low, pool_high))

    columns_in = padded_of(inputs)
    first_pre = apply_flat(columns_in, first_fwd)
    hidden = inputs + jax.nn.silu(first_pre)
    columns_hidden = padded_of(hidden)
    second_pre = apply_flat(columns_hidden, second_fwd)
    outputs = hidden + jax.nn.silu(second_pre)
    second_err = upstream * slope(second_pre)
    hidden_grad = upstream + apply_flat(padded_of(second_err), second_back)
    second_local = kernel_terms(columns_hidden, second_err.astype(jnp.bfloat16))
    first_err = hidden_grad * slope(first_pre)
    input_grad = hidden_grad + apply_flat(padded_of(first_err), first_back)
    first_local = kernel_terms(columns_in, first_err.astype(jnp.bfloat16))
    first_total, second_total = lax.psum((first_local, second_local), ("brick", "scene"))
    total_slots = (
        lax.axis_size("brick") * lax.axis_size("scene") * scenes_here * slots_here * voxels
    )
    scale = 1.0 / jnp.sqrt(jnp.float32(total_slots))
    return (outputs, input_grad, first_total * scale, second_total * scale)


def solution(mesh):
    return jax.shard_map(
        body,
        mesh=mesh,
        in_specs=(
            P("scene", "brick", None, None),
            P("scene", "brick", None, None),
            P(),
            P(),
            P("brick"),
            P("brick", None),
        ),
        out_specs=(P("scene", "brick", None, None), P("scene", "brick", None, None), P(), P()),
        check_vma=False,
    )
```

profile of v0, /device:TPU:2, one launch (start us, length us, event | category | flops | bytes accessed | tf_op | source)
XLA Modules:
  0.0 656.1 jit_solution(11767349416236179653)
XLA Ops:
  9.2 4.2 collective-permute-start.1
  68.2 2.7 maximum_maximum_fusion.5
  72.3 2.0 maximum_maximum_fusion
  75.6 2.0 copy.455
  80.4 3.3 fusion.271
  88.4 2.5 fusion.263
  91.0 2.0 copy.447
  93.0 2.0 copy.446
  105.5 2.3 fusion.262
  126.8 2.2 copy-done
  129.1 3.3 fusion.254
  132.5 4.6 collective-permute-start.3
  137.1 2.1 collective-permute-start.2
  166.9 2.5 maximum_maximum_fusion.7
  170.8 2.4 maximum_maximum_fusion.1
  179.3 3.3 fusion.269
  182.6 2.0 copy.521
  187.3 2.5 fusion.261
  189.9 2.0 copy.518
  204.3 2.3 fusion.260
  226.0 3.9 multiply_convert_fusion.1
  230.0 3.8 fusion.4
  233.9 3.9 collective-permute-start.5
  237.8 2.1 collective-permute-start.4
  267.5 2.5 maximum_maximum_fusion.9
  271.4 2.2 maximum_maximum_fusion.2
  279.7 3.3 fusion.267
  285.0 2.0 copy.591
  287.9 2.5 fusion.259
  290.4 2.0 copy.589
  304.8 2.3 fusion.258
  344.2 3.7 copy.607
  347.9 3.4 multiply_convert_fusion
  351.4 2.9 fusion.7
  354.4 3.9 collective-permute-start.7
  358.3 4.1 collective-permute-start.6
  389.6 2.5 maximum_maximum_fusion.11
  393.5 2.0 maximum_maximum_fusion.3
  401.6 3.4 fusion.265
  409.9 2.6 fusion.257
  412.5 2.0 copy.660
  414.5 2.0 copy.659
  416.5 2.0 copy.658
  427.0 2.4 fusion.256
  448.5 3.2 fusion.11
  451.7 192.7 %all-reduce.3.cloned.1.call-done = (f32[27,64,64]{2,1,0:T(8,128)}, f32[27,64,64]{2,1,0:T(8,128)}) async-done(((f32[27,64,64]{2,1,0:T(8,128)}, f32[27,64,64]{2,1,0:T(8,128)}), (f32[27,64,64]{2,1,0:T(8,128)}, f32[27,64,64]{2,1,0:T(8,128)})) %all-reduce.3.cloned.1.call-update) | async-done | bytes 884752 | tf_op jit(solution)/shard_map/psum | solution.py:129
  644.4 2.2 broadcast_multiply_fusion.1
  646.6 2.2 broadcast_multiply_fusion
  (1395 shorter events, 313.9 us)
Async XLA Ops:
  7.2 25.6 %copy-start.98 = (f32[27,64,64]{2,1,0:T(8,128)S(1)}, f32[27,64,64]{2,1,0:T(8,128)}, u32[]{:S(2)}) copy-start(f32[27,64,64]{2,1,0:T(8,128)} %param.22) | copy-start | bytes 1327108
  7.2 25.7 %copy-start.99 = (f32[27,64,64]{2,1,0:T(8,128)S(1)}, f32[27,64,64]{2,1,0:T(8,128)}, u32[]{:S(2)}) copy-start(f32[27,64,64]{2,1,0:T(8,128)} %param.23) | copy-start | bytes 1327108
  7.2 637.2 %all-reduce.3.cloned.1.call-start = ((), (), s32[]{:S(2)}) async-start(), calls=%async_computation | async-start | bytes 3538944 | tf_op jit(solution)/shard_map/psum | solution.py:129
  9.2 40.3 %collective-permute-start.1 = (bf16[1,4,64,512]{3,2,1,0:T(8,128)(2,1)S(1)}, bf16[1,4,64,512]{3,2,1,0:T(8,128)(2,1)}, u32[]{:S(2)}, u32[]{:S(2)}) collective-permute-start(bf16[1,4,64,512]{3,2,1,0:T(8,128)(2,1)S(1)} %multiply_convert_fusion.2), channel_id=1, source_target_pairs={{8,0},{16,8},{24,16},{32,24},{40,32},{48,40},{56,48},{64,56},{72,6... | collective-permute-start | bytes 786440 | tf_op jit(solution)/shard_map/ppermute | solution.py:19
  13.3 34.3 %collective-permute-start = (bf16[1,4,64,512]{3,2,1,0:T(8,128)(2,1)S(1)}, bf16[1,4,64,512]{3,2,1,0:T(8,128)(2,1)}, u32[]{:S(2)}, u32[]{:S(2)}) collective-permute-start(bf16[1,4,64,512]{3,2,1,0:T(8,128)(2,1)S(1)} %multiply_convert_fusion.2), channel_id=1, source_target_pairs={{0,8},{8,16},{16,24},{24,32},{32,40},{40,48},{48,56},{56,64},{64,7... | collective-permute-start | bytes 786440 | tf_op jit(solution)/shard_map/ppermute | solution.py:18
  19.3 37.3 %copy-start.233 = (pred[4]{0:T(512)(128)(4,1)}, pred[4]{0:T(512)(128)(4,1)S(1)}, u32[]{:S(2)}) copy-start(pred[4]{0:T(512)(128)(4,1)S(1)} %get-tuple-element.336) | copy-start | bytes 16
  20.3 21.8 %copy-start.329 = (pred[4]{0:T(512)(128)(4,1)}, pred[4]{0:T(512)(128)(4,1)S(1)}, u32[]{:S(2)}) copy-start(pred[4]{0:T(512)(128)(4,1)S(1)} %compare_and_fusion.24) | copy-start | bytes 16
  20.9 19.8 %copy-start.253 = (pred[4]{0:T(512)(128)(4,1)}, pred[4]{0:T(512)(128)(4,1)S(1)}, u32[]{:S(2)}) copy-start(pred[4]{0:T(512)(128)(4,1)S(1)} %get-tuple-element.310) | copy-start | bytes 16
  21.4 20.1 %copy-start.249 = (pred[4]{0:T(512)(128)(4,1)}, pred[4]{0:T(512)(128)(4,1)S(1)}, u32[]{:S(2)}) copy-start(pred[4]{0:T(512)(128)(4,1)S(1)} %get-tuple-element.306) | copy-start | bytes 16
  21.9 21.1 %copy-start.153 = (pred[4]{0:T(512)(128)(4,1)}, pred[4]{0:T(512)(128)(4,1)S(1)}, u32[]{:S(2)}) copy-start(pred[4]{0:T(512)(128)(4,1)S(1)} %get-tuple-element.308) | copy-start | bytes 16
  22.5 20.4 %copy-start.157 = (pred[4]{0:T(512)(128)(4,1)}, pred[4]{0:T(512)(128)(4,1)S(1)}, u32[]{:S(2)}) copy-start(pred[4]{0:T(512)(128)(4,1)S(1)} %get-tuple-element.312) | copy-start | bytes 16
  23.7 19.1 %copy-start.165 = (pred[4]{0:T(512)(128)(4,1)}, pred[4]{0:T(512)(128)(4,1)S(1)}, u32[]{:S(2)}) copy-start(pred[4]{0:T(512)(128)(4,1)S(1)} %get-tuple-element.315) | copy-start | bytes 16
  24.2 17.2 %copy-start.257 = (pred[4]{0:T(512)(128)(4,1)}, pred[4]{0:T(512)(128)(4,1)S(1)}, u32[]{:S(2)}) copy-start(pred[4]{0:T(512)(128)(4,1)S(1)} %get-tuple-element.317) | copy-start | bytes 16
  24.8 22.7 %copy-start.161 = (pred[4]{0:T(512)(128)(4,1)}, pred[4]{0:T(512)(128)(4,1)S(1)}, u32[]{:S(2)}) copy-start(pred[4]{0:T(512)(128)(4,1)S(1)} %get-tuple-element.319) | copy-start | bytes 16
  25.6 16.6 %copy-start.177 = (pred[4]{0:T(512)(128)(4,1)}, pred[4]{0:T(512)(128)(4,1)S(1)}, u32[]{:S(2)}) copy-start(pred[4]{0:T(512)(128)(4,1)S(1)} %get-tuple-element.62) | copy-start | bytes 16
  25.6 21.9 %copy-start.121 = (pred[4]{0:T(512)(128)(4,1)}, pred[4]{0:T(512)(128)(4,1)S(1)}, u32[]{:S(2)}) copy-start(pred[4]{0:T(512)(128)(4,1)S(1)} %get-tuple-element.59) | copy-start | bytes 16
  25.6 30.1 %copy-start.173 = (pred[4]{0:T(512)(128)(4,1)}, pred[4]{0:T(512)(128)(4,1)S(1)}, u32[]{:S(2)}) copy-start(pred[4]{0:T(512)(128)(4,1)S(1)} %get-tuple-element.60) | copy-start | bytes 16
  26.6 14.8 %copy-start.209 = (pred[4]{0:T(512)(128)(4,1)}, pred[4]{0:T(512)(128)(4,1)S(1)}, u32[]{:S(2)}) copy-start(pred[4]{0:T(512)(128)(4,1)S(1)} %get-tuple-element.55) | copy-start | bytes 16
  26.6 14.9 %copy-start.205 = (pred[4]{0:T(512)(128)(4,1)}, pred[4]{0:T(512)(128)(4,1)S(1)}, u32[]{:S(2)}) copy-start(pred[4]{0:T(512)(128)(4,1)S(1)} %get-tuple-element.39) | copy-start | bytes 16
  26.6 16.3 %copy-start.141 = (pred[4]{0:T(512)(128)(4,1)}, pred[4]{0:T(512)(128)(4,1)S(1)}, u32[]{:S(2)}) copy-start(pred[4]{0:T(512)(128)(4,1)S(1)} %get-tuple-element.52) | copy-start | bytes 16
  26.6 16.4 %copy-start.137 = (pred[4]{0:T(512)(128)(4,1)}, pred[4]{0:T(512)(128)(4,1)S(1)}, u32[]{:S(2)}) copy-start(pred[4]{0:T(512)(128)(4,1)S(1)} %get-tuple-element.47) | copy-start | bytes 16
  26.6 16.5 %copy-start.133 = (pred[4]{0:T(512)(128)(4,1)}, pred[4]{0:T(512)(128)(4,1)S(1)}, u32[]{:S(2)}) copy-start(pred[4]{0:T(512)(128)(4,1)S(1)} %get-tuple-element.42) | copy-start | bytes 16
  26.6 28.3 %copy-start.201 = (pred[4]{0:T(512)(128)(4,1)}, pred[4]{0:T(512)(128)(4,1)S(1)}, u32[]{:S(2)}) copy-start(pred[4]{0:T(512)(128)(4,1)S(1)} %get-tuple-element.43) | copy-start | bytes 16
  26.6 30.0 %copy-start.197 = (pred[4]{0:T(512)(128)(4,1)}, pred[4]{0:T(512)(128)(4,1)S(1)}, u32[]{:S(2)}) copy-start(pred[4]{0:T(512)(128)(4,1)S(1)} %get-tuple-element.53) | copy-start | bytes 16
  27.9 19.0 %copy-start.321 = (s32[1024]{0:T(1024)}, s32[1024]{0:T(1024)S(1)}, u32[]{:S(2)}) copy-start(s32[1024]{0:T(1024)S(1)} %pad_clamp_fusion.21) | copy-start | bytes 12292
  43.0 28.0 %copy-start.33 = (bf16[1,4,64,8,1,8]{2,5,4,3,1,0:T(8,128)(2,1)}, bf16[1,4,64,8,1,8]{2,5,4,3,1,0:T(8,128)(2,1)S(1)}, u32[]{:S(2)}) copy-start(bf16[1,4,64,8,1,8]{2,5,4,3,1,0:T(8,128)(2,1)S(1)} %fusion.41) | copy-start | bytes 98308
  49.3 15.4 %copy-start.181 = (pred[4]{0:T(512)(128)(4,1)S(1)}, pred[4]{0:T(512)(128)(4,1)}, u32[]{:S(2)}) copy-start(pred[4]{0:T(512)(128)(4,1)} %get-tuple-element.46) | copy-start | bytes 16
  49.3 15.4 %copy-start.217 = (pred[4]{0:T(512)(128)(4,1)S(1)}, pred[4]{0:T(512)(128)(4,1)}, u32[]{:S(2)}) copy-start(pred[4]{0:T(512)(128)(4,1)} %get-tuple-element.311) | copy-start | bytes 16
  50.8 14.8 %copy-start.125 = (pred[4]{0:T(512)(128)(4,1)S(1)}, pred[4]{0:T(512)(128)(4,1)}, u32[]{:S(2)}) copy-start(pred[4]{0:T(512)(128)(4,1)} %get-tuple-element.49) | copy-start | bytes 16
  50.8 14.8 %copy-start.145 = (pred[4]{0:T(512)(128)(4,1)S(1)}, pred[4]{0:T(512)(128)(4,1)}, u32[]{:S(2)}) copy-start(pred[4]{0:T(512)(128)(4,1)} %get-tuple-element.313) | copy-start | bytes 16
  132.5 16.5 %collective-permute-start.3 = (bf16[1,4,64,512]{3,2,1,0:T(8,128)(2,1)}, bf16[1,4,64,512]{3,2,1,0:T(8,128)(2,1)S(1)}, u32[]{:S(2)}, u32[]{:S(2)}) collective-permute-start(bf16[1,4,64,512]{3,2,1,0:T(8,128)(2,1)} %get-tuple-element.285), channel_id=1, source_target_pairs={{8,0},{16,8},{24,16},{32,24},{40,32},{48,40},{56,48},{64,56},{72,6... | collective-permute-start | bytes 786440 | tf_op jit(solution)/shard_map/ppermute | solution.py:19
  137.1 11.0 %collective-permute-start.2 = (bf16[1,4,64,512]{3,2,1,0:T(8,128)(2,1)}, bf16[1,4,64,512]{3,2,1,0:T(8,128)(2,1)S(1)}, u32[]{:S(2)}, u32[]{:S(2)}) collective-permute-start(bf16[1,4,64,512]{3,2,1,0:T(8,128)(2,1)} %get-tuple-element.285), channel_id=1, source_target_pairs={{0,8},{8,16},{16,24},{24,32},{32,40},{40,48},{48,56},{56,64},{64,7... | collective-permute-start | bytes 786440 | tf_op jit(solution)/shard_map/ppermute | solution.py:18
  145.4 24.2 %copy-start.34 = (bf16[1,4,64,8,1,8]{2,5,4,3,1,0:T(8,128)(2,1)}, bf16[1,4,64,8,1,8]{2,5,4,3,1,0:T(8,128)(2,1)S(1)}, u32[]{:S(2)}) copy-start(bf16[1,4,64,8,1,8]{2,5,4,3,1,0:T(8,128)(2,1)S(1)} %fusion.35) | copy-start | bytes 98308
  149.4 14.8 %copy-start.182 = (pred[4]{0:T(512)(128)(4,1)S(1)}, pred[4]{0:T(512)(128)(4,1)}, u32[]{:S(2)}) copy-start(pred[4]{0:T(512)(128)(4,1)} %get-tuple-element.46) | copy-start | bytes 16
  149.4 14.8 %copy-start.218 = (pred[4]{0:T(512)(128)(4,1)S(1)}, pred[4]{0:T(512)(128)(4,1)}, u32[]{:S(2)}) copy-start(pred[4]{0:T(512)(128)(4,1)} %get-tuple-element.311) | copy-start | bytes 16
  233.9 15.8 %collective-permute-start.5 = (bf16[1,4,64,512]{3,2,1,0:T(8,128)(2,1)}, bf16[1,4,64,512]{3,2,1,0:T(8,128)(2,1)S(1)}, u32[]{:S(2)}, u32[]{:S(2)}) collective-permute-start(bf16[1,4,64,512]{3,2,1,0:T(8,128)(2,1)} %get-tuple-element.171), channel_id=1, source_target_pairs={{8,0},{16,8},{24,16},{32,24},{40,32},{48,40},{56,48},{64,56},{72,6... | collective-permute-start | bytes 786440 | tf_op jit(solution)/shard_map/ppermute | solution.py:19
  237.8 11.0 %collective-permute-start.4 = (bf16[1,4,64,512]{3,2,1,0:T(8,128)(2,1)}, bf16[1,4,64,512]{3,2,1,0:T(8,128)(2,1)S(1)}, u32[]{:S(2)}, u32[]{:S(2)}) collective-permute-start(bf16[1,4,64,512]{3,2,1,0:T(8,128)(2,1)} %get-tuple-element.171), channel_id=1, source_target_pairs={{0,8},{8,16},{16,24},{24,32},{32,40},{40,48},{48,56},{56,64},{64,7... | collective-permute-start | bytes 786440 | tf_op jit(solution)/shard_map/ppermute | solution.py:18
  246.0 24.1 %copy-start.35 = (bf16[1,4,64,8,1,8]{2,5,4,3,1,0:T(8,128)(2,1)}, bf16[1,4,64,8,1,8]{2,5,4,3,1,0:T(8,128)(2,1)S(1)}, u32[]{:S(2)}) copy-start(bf16[1,4,64,8,1,8]{2,5,4,3,1,0:T(8,128)(2,1)S(1)} %fusion.29) | copy-start | bytes 98308
  250.1 14.8 %copy-start.183 = (pred[4]{0:T(512)(128)(4,1)S(1)}, pred[4]{0:T(512)(128)(4,1)}, u32[]{:S(2)}) copy-start(pred[4]{0:T(512)(128)(4,1)} %get-tuple-element.46) | copy-start | bytes 16
  250.1 14.8 %copy-start.219 = (pred[4]{0:T(512)(128)(4,1)S(1)}, pred[4]{0:T(512)(128)(4,1)}, u32[]{:S(2)}) copy-start(pred[4]{0:T(512)(128)(4,1)} %get-tuple-element.311) | copy-start | bytes 16
  315.8 15.1 %copy-start.62 = (bf16[1,4,1,64,512]{4,3,1,2,0:T(8,128)(2,1)S(1)}, bf16[1,4,1,64,512]{4,3,1,2,0:T(8,128)(2,1)}, u32[]{:S(2)}) copy-start(bf16[1,4,1,64,512]{4,3,1,2,0:T(8,128)(2,1)} %copy.591) | copy-start | bytes 786436
  316.7 14.9 %copy-start.58 = (bf16[1,4,1,64,512]{4,3,1,2,0:T(8,128)(2,1)S(1)}, bf16[1,4,1,64,512]{4,3,1,2,0:T(8,128)(2,1)}, u32[]{:S(2)}) copy-start(bf16[1,4,1,64,512]{4,3,1,2,0:T(8,128)(2,1)} %copy.592) | copy-start | bytes 786436
  354.3 14.7 %copy-start.180 = (pred[4]{0:T(512)(128)(4,1)S(1)}, pred[4]{0:T(512)(128)(4,1)}, u32[]{:S(2)}) copy-start(pred[4]{0:T(512)(128)(4,1)} %copy-done.177) | copy-start | bytes 16
  354.4 17.4 %collective-permute-start.7 = (bf16[1,4,64,512]{3,2,1,0:T(8,128)(2,1)S(1)}, bf16[1,4,64,512]{3,2,1,0:T(8,128)(2,1)S(1)}, u32[]{:S(2)}, u32[]{:S(2)}) collective-permute-start(bf16[1,4,64,512]{3,2,1,0:T(8,128)(2,1)S(1)} %get-tuple-element.287), channel_id=1, source_target_pairs={{8,0},{16,8},{24,16},{32,24},{40,32},{48,40},{56,48},{64,56},{72,6... | collective-permute-start | bytes 786440 | tf_op jit(solution)/shard_map/ppermute | solution.py:19
  358.3 12.6 %collective-permute-start.6 = (bf16[1,4,64,512]{3,2,1,0:T(8,128)(2,1)S(1)}, bf16[1,4,64,512]{3,2,1,0:T(8,128)(2,1)S(1)}, u32[]{:S(2)}, u32[]{:S(2)}) collective-permute-start(bf16[1,4,64,512]{3,2,1,0:T(8,128)(2,1)S(1)} %get-tuple-element.287), channel_id=1, source_target_pairs={{0,8},{8,16},{16,24},{24,32},{32,40},{40,48},{48,56},{56,64},{64,7... | collective-permute-start | bytes 786440 | tf_op jit(solution)/shard_map/ppermute | solution.py:18
  368.2 24.0 %copy-start.32 = (bf16[1,4,64,8,1,8]{2,5,4,3,1,0:T(8,128)(2,1)}, bf16[1,4,64,8,1,8]{2,5,4,3,1,0:T(8,128)(2,1)S(1)}, u32[]{:S(2)}) copy-start(bf16[1,4,64,8,1,8]{2,5,4,3,1,0:T(8,128)(2,1)S(1)} %fusion.23) | copy-start | bytes 98308
  372.1 14.8 %copy-start.184 = (pred[4]{0:T(512)(128)(4,1)S(1)}, pred[4]{0:T(512)(128)(4,1)}, u32[]{:S(2)}) copy-start(pred[4]{0:T(512)(128)(4,1)} %get-tuple-element.46) | copy-start | bytes 16
  372.1 14.8 %copy-start.220 = (pred[4]{0:T(512)(128)(4,1)S(1)}, pred[4]{0:T(512)(128)(4,1)}, u32[]{:S(2)}) copy-start(pred[4]{0:T(512)(128)(4,1)} %get-tuple-element.311) | copy-start | bytes 16
  (304 other events, 2625.2 us)
Sparse Core Ops, SparseCore 0:
  370.8 273.5 all-reduce.2
where the time goes:
time: 667 us; the launch traced here: 656 us
  local copies, waits for them, and re-layouts  330 us (49%)
  waiting for transfers between devices  193 us (29%)
  other arithmetic  63.3 us (9%)
  starting transfers between devices  26.9 us (4%)
  between operations  22.1 us (3%)
  matrix products  20.5 us (3%)
    psum x1, waiting for transfers between devices, body(): lax.psum((first_local, second_local), ('brick', 'scene'))  193 us
    another operation x112, local copies, waits for them, and re-layouts, columns_of(): joined = jnp.stack(stacked, axis=2)  148 us
    gather x104, local copies, waits for them, and re-layouts, assemble(): picked = jnp.take(slab_part, chosen_rows, axis=0)  70.4 us
    unnamed x805, local copies, waits for them, and re-layouts  57.1 us
    slice x16, local copies, waits for them, and re-layouts, columns_of(): part = padded[..., 1 + a:1 + a + E, 1 + b:1 + b + E, 1 + c:1 + c + E]  38.4 us
    ppermute x4, starting transfers between devices, with_halo(): after = lax.ppermute(first, axis, down)  16.6 us
    dot_general x4, matrix products, apply_flat(): jnp.einsum('ko,nskp->nsop', weight_flat, columns, preferred_element_type=...  13.8 us
  transfers between devices with their start and end apart: 9, of which 1 were waited for; matrix products, arithmetic and copies ran while one was open for 21% of the time, Pallas kernels for 0%

commit v1 on v0

--- a/solution.py
+++ b/solution.py
@@ -126,7 +126,7 @@
     first_err = hidden_grad * slope(first_pre)
     input_grad = hidden_grad + apply_flat(padded_of(first_err), first_back)
     first_local = kernel_terms(columns_in, first_err.astype(jnp.bfloat16))
-    first_total, second_total = lax.psum((first_local, second_local), ("brick", "scene"))
+    first_total, second_total = lax.psum(lax.psum((first_local, second_local), "brick"), "scene")
     total_slots = (
         lax.axis_size("brick") * lax.axis_size("scene") * scenes_here * slots_here * voxels
     )

time: 667 us -> 627 us (0.940)
  waiting for transfers between devices: 193 us -> 127 us
  local copies, waits for them, and re-layouts: 330 us -> 354 us
    psum x1 -> x2, waiting for transfers between devices: 193 us -> 127 us  [the longest x1 65.7 us: body(): lax.psum(lax.psum((first_local, second_local), 'brick'), 'scene')]
    unnamed x805 -> x797, local copies, waits for them, and re-layouts: 57.1 us -> 76.6 us
  transfers between devices with their start and end apart: 9 -> 10, of which waited for: 1 -> 2; matrix products, arithmetic and copies ran while one was open for 21% -> 27% of each run, Pallas kernels for 0% -> 0%
where the time goes in v1:
time: 627 us; the launch traced here: 616 us
  local copies, waits for them, and re-layouts  354 us (56%)
  waiting for transfers between devices  127 us (20%)
  other arithmetic  63.2 us (10%)
  starting transfers between devices  27 us (4%)
  matrix products  22.5 us (4%)
  between operations  21.8 us (3%)
    another operation x112, local copies, waits for them, and re-layouts, columns_of(): joined = jnp.stack(stacked, axis=2)  153 us
    unnamed x797, local copies, waits for them, and re-layouts  76.6 us
    gather x104, local copies, waits for them, and re-layouts, assemble(): picked = jnp.take(slab_part, chosen_rows, axis=0)  70.4 us
    psum x1, waiting for transfers between devices, body(): lax.psum(lax.psum((first_local, second_local), 'brick'), 'scene')  65.7 us
    psum x1, waiting for transfers between devices, body(): lax.psum((first_local, second_local), 'brick')  61 us
    slice x16, local copies, waits for them, and re-layouts, columns_of(): part = padded[..., 1 + a:1 + a + E, 1 + b:1 + b + E, 1 + c:1 + c + E]  38.2 us
    ppermute x4, starting transfers between devices, with_halo(): after = lax.ppermute(first, axis, down)  16.6 us
    dot_general x4, matrix products, apply_flat(): jnp.einsum('ko,nskp->nsop', weight_flat, columns, preferred_element_type=...  15.8 us
  transfers between devices with their start and end apart: 10, of which 2 were waited for; matrix products, arithmetic and copies ran while one was open for 27% of the time, Pallas kernels for 0%

profile of v1, /device:TPU:2, one launch (start us, length us, event | category | flops | bytes accessed | tf_op | source)
XLA Modules:
  0.0 615.5 jit_solution(1048332697748318546)
XLA Ops:
  9.2 4.2 collective-permute-start.1
  68.1 2.7 maximum_maximum_fusion.5
  72.2 2.0 maximum_maximum_fusion
  80.3 3.3 fusion.271
  88.3 2.5 fusion.263
  90.9 2.0 copy.447
  105.4 2.3 fusion.262
  126.8 2.2 copy-done
  129.0 3.3 fusion.254
  132.4 4.6 collective-permute-start.3
  137.1 2.1 collective-permute-start.2
  166.8 2.5 maximum_maximum_fusion.7
  170.7 2.4 maximum_maximum_fusion.1
  179.2 3.3 fusion.269
  187.3 2.5 fusion.261
  189.8 2.0 copy.518
  204.2 2.3 fusion.260
  226.0 3.9 multiply_convert_fusion.1
  229.9 3.8 fusion.4
  233.8 3.9 collective-permute-start.5
  237.8 2.1 collective-permute-start.4
  267.5 2.5 maximum_maximum_fusion.9
  271.3 2.2 maximum_maximum_fusion.2
  279.7 3.4 fusion.267
  287.9 2.5 fusion.259
  290.4 2.0 copy.589
  304.8 2.3 fusion.258
  344.2 3.7 copy.607
  347.9 3.4 multiply_convert_fusion
  351.4 2.9 fusion.7
  354.3 3.9 collective-permute-start.7
  358.3 4.1 collective-permute-start.6
  389.6 2.5 maximum_maximum_fusion.11
  393.5 2.0 maximum_maximum_fusion.3
  396.8 2.0 copy.668
  401.6 3.3 fusion.265
  409.7 2.5 fusion.257
  412.3 2.0 copy.660
  418.2 2.0 copy.657
  420.2 2.0 copy.656
  426.8 2.3 fusion.256
  430.3 2.0 copy.669
  465.0 6.9 %copy.678 = bf16[1,4,27,64,512]{4,3,2,1,0:T(8,128)(2,1)} copy(bf16[1,4,27,64,512]{4,3,1,2,0:T(8,128)(2,1)} %constant_dynamic-update-slice_fusion.78) | data formatting | bytes 14155776 | tf_op jit(solution)/shard_map/stack | solution.py:65
  471.9 61.0 %all-reduce.5.cloned.1.call-done = (f32[27,64,64]{2,1,0:T(8,128)}, f32[27,64,64]{2,1,0:T(8,128)}) async-done(((f32[27,64,64]{2,1,0:T(8,128)}, f32[27,64,64]{2,1,0:T(8,128)}), (f32[27,64,64]{2,1,0:T(8,128)}, f32[27,64,64]{2,1,0:T(8,128)})) %all-reduce.5.cloned.1.call-update) | async-done | bytes 884752 | tf_op jit(solution)/shard_map/psum | solution.py:129
  533.0 5.1 fusion.11
  538.1 65.7 %all-reduce.7.cloned.1.call-done = (f32[27,64,64]{2,1,0:T(8,128)}, f32[27,64,64]{2,1,0:T(8,128)}) async-done(((f32[27,64,64]{2,1,0:T(8,128)}, f32[27,64,64]{2,1,0:T(8,128)}), (f32[27,64,64]{2,1,0:T(8,128)}, f32[27,64,64]{2,1,0:T(8,128)})) %all-reduce.7.cloned.1.call-update) | async-done | bytes 884752 | tf_op jit(solution)/shard_map/psum | solution.py:129
  603.8 2.2 broadcast_multiply_fusion.1
  606.0 2.2 broadcast_multiply_fusion
  (1390 shorter events, 334.7 us)
Async XLA Ops:
  7.2 25.4 %copy-start.94 = (f32[27,64,64]{2,1,0:T(8,128)S(1)}, f32[27,64,64]{2,1,0:T(8,128)}, u32[]{:S(2)}) copy-start(f32[27,64,64]{2,1,0:T(8,128)} %param.22) | copy-start | bytes 1327108
  7.2 25.5 %copy-start.95 = (f32[27,64,64]{2,1,0:T(8,128)S(1)}, f32[27,64,64]{2,1,0:T(8,128)}, u32[]{:S(2)}) copy-start(f32[27,64,64]{2,1,0:T(8,128)} %param.23) | copy-start | bytes 1327108
  7.2 525.7 %all-reduce.5.cloned.1.call-start = ((), (), s32[]{:S(2)}) async-start(), calls=%async_computation | async-start | bytes 3538944 | tf_op jit(solution)/shard_map/psum | solution.py:129
  9.2 40.1 %collective-permute-start.1 = (bf16[1,4,64,512]{3,2,1,0:T(8,128)(2,1)S(1)}, bf16[1,4,64,512]{3,2,1,0:T(8,128)(2,1)}, u32[]{:S(2)}, u32[]{:S(2)}) collective-permute-start(bf16[1,4,64,512]{3,2,1,0:T(8,128)(2,1)S(1)} %multiply_convert_fusion.2), channel_id=1, source_target_pairs={{8,0},{16,8},{24,16},{32,24},{40,32},{48,40},{56,48},{64,56},{72,6... | collective-permute-start | bytes 786440 | tf_op jit(solution)/shard_map/ppermute | solution.py:19
  13.3 34.1 %collective-permute-start = (bf16[1,4,64,512]{3,2,1,0:T(8,128)(2,1)S(1)}, bf16[1,4,64,512]{3,2,1,0:T(8,128)(2,1)}, u32[]{:S(2)}, u32[]{:S(2)}) collective-permute-start(bf16[1,4,64,512]{3,2,1,0:T(8,128)(2,1)S(1)} %multiply_convert_fusion.2), channel_id=1, source_target_pairs={{0,8},{8,16},{16,24},{24,32},{32,40},{40,48},{48,56},{56,64},{64,7... | collective-permute-start | bytes 786440 | tf_op jit(solution)/shard_map/ppermute | solution.py:18
  19.2 37.3 %copy-start.229 = (pred[4]{0:T(512)(128)(4,1)}, pred[4]{0:T(512)(128)(4,1)S(1)}, u32[]{:S(2)}) copy-start(pred[4]{0:T(512)(128)(4,1)S(1)} %get-tuple-element.338) | copy-start | bytes 16
  20.2 21.8 %copy-start.325 = (pred[4]{0:T(512)(128)(4,1)}, pred[4]{0:T(512)(128)(4,1)S(1)}, u32[]{:S(2)}) copy-start(pred[4]{0:T(512)(128)(4,1)S(1)} %compare_and_fusion.24) | copy-start | bytes 16
  20.8 19.7 %copy-start.249 = (pred[4]{0:T(512)(128)(4,1)}, pred[4]{0:T(512)(128)(4,1)S(1)}, u32[]{:S(2)}) copy-start(pred[4]{0:T(512)(128)(4,1)S(1)} %get-tuple-element.312) | copy-start | bytes 16
  21.3 20.0 %copy-start.245 = (pred[4]{0:T(512)(128)(4,1)}, pred[4]{0:T(512)(128)(4,1)S(1)}, u32[]{:S(2)}) copy-start(pred[4]{0:T(512)(128)(4,1)S(1)} %get-tuple-element.308) | copy-start | bytes 16
  21.9 21.0 %copy-start.149 = (pred[4]{0:T(512)(128)(4,1)}, pred[4]{0:T(512)(128)(4,1)S(1)}, u32[]{:S(2)}) copy-start(pred[4]{0:T(512)(128)(4,1)S(1)} %get-tuple-element.310) | copy-start | bytes 16
  22.4 20.4 %copy-start.157 = (pred[4]{0:T(512)(128)(4,1)}, pred[4]{0:T(512)(128)(4,1)S(1)}, u32[]{:S(2)}) copy-start(pred[4]{0:T(512)(128)(4,1)S(1)} %get-tuple-element.314) | copy-start | bytes 16
  23.5 19.2 %copy-start.161 = (pred[4]{0:T(512)(128)(4,1)}, pred[4]{0:T(512)(128)(4,1)S(1)}, u32[]{:S(2)}) copy-start(pred[4]{0:T(512)(128)(4,1)S(1)} %get-tuple-element.317) | copy-start | bytes 16
  24.0 17.2 %copy-start.253 = (pred[4]{0:T(512)(128)(4,1)}, pred[4]{0:T(512)(128)(4,1)S(1)}, u32[]{:S(2)}) copy-start(pred[4]{0:T(512)(128)(4,1)S(1)} %get-tuple-element.319) | copy-start | bytes 16
  24.6 22.7 %copy-start.153 = (pred[4]{0:T(512)(128)(4,1)}, pred[4]{0:T(512)(128)(4,1)S(1)}, u32[]{:S(2)}) copy-start(pred[4]{0:T(512)(128)(4,1)S(1)} %get-tuple-element.321) | copy-start | bytes 16
  25.4 16.6 %copy-start.173 = (pred[4]{0:T(512)(128)(4,1)}, pred[4]{0:T(512)(128)(4,1)S(1)}, u32[]{:S(2)}) copy-start(pred[4]{0:T(512)(128)(4,1)S(1)} %get-tuple-element.62) | copy-start | bytes 16
  25.4 22.0 %copy-start.117 = (pred[4]{0:T(512)(128)(4,1)}, pred[4]{0:T(512)(128)(4,1)S(1)}, u32[]{:S(2)}) copy-start(pred[4]{0:T(512)(128)(4,1)S(1)} %get-tuple-element.59) | copy-start | bytes 16
  25.4 30.2 %copy-start.169 = (pred[4]{0:T(512)(128)(4,1)}, pred[4]{0:T(512)(128)(4,1)S(1)}, u32[]{:S(2)}) copy-start(pred[4]{0:T(512)(128)(4,1)S(1)} %get-tuple-element.60) | copy-start | bytes 16
  26.4 14.8 %copy-start.205 = (pred[4]{0:T(512)(128)(4,1)}, pred[4]{0:T(512)(128)(4,1)S(1)}, u32[]{:S(2)}) copy-start(pred[4]{0:T(512)(128)(4,1)S(1)} %get-tuple-element.55) | copy-start | bytes 16
  26.4 14.9 %copy-start.201 = (pred[4]{0:T(512)(128)(4,1)}, pred[4]{0:T(512)(128)(4,1)S(1)}, u32[]{:S(2)}) copy-start(pred[4]{0:T(512)(128)(4,1)S(1)} %get-tuple-element.39) | copy-start | bytes 16
  26.4 16.3 %copy-start.137 = (pred[4]{0:T(512)(128)(4,1)}, pred[4]{0:T(512)(128)(4,1)S(1)}, u32[]{:S(2)}) copy-start(pred[4]{0:T(512)(128)(4,1)S(1)} %get-tuple-element.52) | copy-start | bytes 16
  26.4 16.4 %copy-start.133 = (pred[4]{0:T(512)(128)(4,1)}, pred[4]{0:T(512)(128)(4,1)S(1)}, u32[]{:S(2)}) copy-start(pred[4]{0:T(512)(128)(4,1)S(1)} %get-tuple-element.47) | copy-start | bytes 16
  26.4 16.5 %copy-start.129 = (pred[4]{0:T(512)(128)(4,1)}, pred[4]{0:T(512)(128)(4,1)S(1)}, u32[]{:S(2)}) copy-start(pred[4]{0:T(512)(128)(4,1)S(1)} %get-tuple-element.42) | copy-start | bytes 16
  26.4 28.3 %copy-start.197 = (pred[4]{0:T(512)(128)(4,1)}, pred[4]{0:T(512)(128)(4,1)S(1)}, u32[]{:S(2)}) copy-start(pred[4]{0:T(512)(128)(4,1)S(1)} %get-tuple-element.43) | copy-start | bytes 16
  26.4 30.0 %copy-start.193 = (pred[4]{0:T(512)(128)(4,1)}, pred[4]{0:T(512)(128)(4,1)S(1)}, u32[]{:S(2)}) copy-start(pred[4]{0:T(512)(128)(4,1)S(1)} %get-tuple-element.53) | copy-start | bytes 16
  27.7 19.1 %copy-start.317 = (s32[1024]{0:T(1024)}, s32[1024]{0:T(1024)S(1)}, u32[]{:S(2)}) copy-start(s32[1024]{0:T(1024)S(1)} %pad_clamp_fusion.21) | copy-start | bytes 12292
  42.9 28.0 %copy-start.34 = (bf16[1,4,64,8,1,8]{2,5,4,3,1,0:T(8,128)(2,1)}, bf16[1,4,64,8,1,8]{2,5,4,3,1,0:T(8,128)(2,1)S(1)}, u32[]{:S(2)}) copy-start(bf16[1,4,64,8,1,8]{2,5,4,3,1,0:T(8,128)(2,1)S(1)} %fusion.41) | copy-start | bytes 98308
  49.2 15.4 %copy-start.177 = (pred[4]{0:T(512)(128)(4,1)S(1)}, pred[4]{0:T(512)(128)(4,1)}, u32[]{:S(2)}) copy-start(pred[4]{0:T(512)(128)(4,1)} %get-tuple-element.46) | copy-start | bytes 16
  49.2 15.4 %copy-start.213 = (pred[4]{0:T(512)(128)(4,1)S(1)}, pred[4]{0:T(512)(128)(4,1)}, u32[]{:S(2)}) copy-start(pred[4]{0:T(512)(128)(4,1)} %get-tuple-element.313) | copy-start | bytes 16
  50.6 14.8 %copy-start.121 = (pred[4]{0:T(512)(128)(4,1)S(1)}, pred[4]{0:T(512)(128)(4,1)}, u32[]{:S(2)}) copy-start(pred[4]{0:T(512)(128)(4,1)} %get-tuple-element.49) | copy-start | bytes 16
  132.4 16.5 %collective-permute-start.3 = (bf16[1,4,64,512]{3,2,1,0:T(8,128)(2,1)}, bf16[1,4,64,512]{3,2,1,0:T(8,128)(2,1)S(1)}, u32[]{:S(2)}, u32[]{:S(2)}) collective-permute-start(bf16[1,4,64,512]{3,2,1,0:T(8,128)(2,1)} %get-tuple-element.287), channel_id=1, source_target_pairs={{8,0},{16,8},{24,16},{32,24},{40,32},{48,40},{56,48},{64,56},{72,6... | collective-permute-start | bytes 786440 | tf_op jit(solution)/shard_map/ppermute | solution.py:19
  137.1 11.0 %collective-permute-start.2 = (bf16[1,4,64,512]{3,2,1,0:T(8,128)(2,1)}, bf16[1,4,64,512]{3,2,1,0:T(8,128)(2,1)S(1)}, u32[]{:S(2)}, u32[]{:S(2)}) collective-permute-start(bf16[1,4,64,512]{3,2,1,0:T(8,128)(2,1)} %get-tuple-element.287), channel_id=1, source_target_pairs={{0,8},{8,16},{16,24},{24,32},{32,40},{40,48},{48,56},{56,64},{64,7... | collective-permute-start | bytes 786440 | tf_op jit(solution)/shard_map/ppermute | solution.py:18
  145.3 24.1 %copy-start.35 = (bf16[1,4,64,8,1,8]{2,5,4,3,1,0:T(8,128)(2,1)}, bf16[1,4,64,8,1,8]{2,5,4,3,1,0:T(8,128)(2,1)S(1)}, u32[]{:S(2)}) copy-start(bf16[1,4,64,8,1,8]{2,5,4,3,1,0:T(8,128)(2,1)S(1)} %fusion.35) | copy-start | bytes 98308
  233.8 15.8 %collective-permute-start.5 = (bf16[1,4,64,512]{3,2,1,0:T(8,128)(2,1)}, bf16[1,4,64,512]{3,2,1,0:T(8,128)(2,1)S(1)}, u32[]{:S(2)}, u32[]{:S(2)}) collective-permute-start(bf16[1,4,64,512]{3,2,1,0:T(8,128)(2,1)} %get-tuple-element.173), channel_id=1, source_target_pairs={{8,0},{16,8},{24,16},{32,24},{40,32},{48,40},{56,48},{64,56},{72,6... | collective-permute-start | bytes 786440 | tf_op jit(solution)/shard_map/ppermute | solution.py:19
  237.8 11.0 %collective-permute-start.4 = (bf16[1,4,64,512]{3,2,1,0:T(8,128)(2,1)}, bf16[1,4,64,512]{3,2,1,0:T(8,128)(2,1)S(1)}, u32[]{:S(2)}, u32[]{:S(2)}) collective-permute-start(bf16[1,4,64,512]{3,2,1,0:T(8,128)(2,1)} %get-tuple-element.173), channel_id=1, source_target_pairs={{0,8},{8,16},{16,24},{24,32},{32,40},{40,48},{48,56},{56,64},{64,7... | collective-permute-start | bytes 786440 | tf_op jit(solution)/shard_map/ppermute | solution.py:18
  246.0 24.1 %copy-start.36 = (bf16[1,4,64,8,1,8]{2,5,4,3,1,0:T(8,128)(2,1)}, bf16[1,4,64,8,1,8]{2,5,4,3,1,0:T(8,128)(2,1)S(1)}, u32[]{:S(2)}) copy-start(bf16[1,4,64,8,1,8]{2,5,4,3,1,0:T(8,128)(2,1)S(1)} %fusion.29) | copy-start | bytes 98308
  315.8 15.1 %copy-start.62 = (bf16[1,4,1,64,512]{4,3,1,2,0:T(8,128)(2,1)S(1)}, bf16[1,4,1,64,512]{4,3,1,2,0:T(8,128)(2,1)}, u32[]{:S(2)}) copy-start(bf16[1,4,1,64,512]{4,3,1,2,0:T(8,128)(2,1)} %copy.591) | copy-start | bytes 786436
  316.7 14.9 %copy-start.59 = (bf16[1,4,1,64,512]{4,3,1,2,0:T(8,128)(2,1)S(1)}, bf16[1,4,1,64,512]{4,3,1,2,0:T(8,128)(2,1)}, u32[]{:S(2)}) copy-start(bf16[1,4,1,64,512]{4,3,1,2,0:T(8,128)(2,1)} %copy.592) | copy-start | bytes 786436
  354.3 17.4 %collective-permute-start.7 = (bf16[1,4,64,512]{3,2,1,0:T(8,128)(2,1)S(1)}, bf16[1,4,64,512]{3,2,1,0:T(8,128)(2,1)S(1)}, u32[]{:S(2)}, u32[]{:S(2)}) collective-permute-start(bf16[1,4,64,512]{3,2,1,0:T(8,128)(2,1)S(1)} %get-tuple-element.289), channel_id=1, source_target_pairs={{8,0},{16,8},{24,16},{32,24},{40,32},{48,40},{56,48},{64,56},{72,6... | collective-permute-start | bytes 786440 | tf_op jit(solution)/shard_map/ppermute | solution.py:19
  358.3 12.6 %collective-permute-start.6 = (bf16[1,4,64,512]{3,2,1,0:T(8,128)(2,1)S(1)}, bf16[1,4,64,512]{3,2,1,0:T(8,128)(2,1)S(1)}, u32[]{:S(2)}, u32[]{:S(2)}) collective-permute-start(bf16[1,4,64,512]{3,2,1,0:T(8,128)(2,1)S(1)} %get-tuple-element.289), channel_id=1, source_target_pairs={{0,8},{8,16},{16,24},{24,32},{32,40},{40,48},{48,56},{56,64},{64,7... | collective-permute-start | bytes 786440 | tf_op jit(solution)/shard_map/ppermute | solution.py:18
  368.2 24.1 %copy-start.33 = (bf16[1,4,64,8,1,8]{2,5,4,3,1,0:T(8,128)(2,1)}, bf16[1,4,64,8,1,8]{2,5,4,3,1,0:T(8,128)(2,1)S(1)}, u32[]{:S(2)}) copy-start(bf16[1,4,64,8,1,8]{2,5,4,3,1,0:T(8,128)(2,1)S(1)} %fusion.23) | copy-start | bytes 98308
  370.7 233.1 %all-reduce.7.cloned.1.call-start = ((), (), s32[]{:S(2)}) async-start(), calls=%async_computation.1 | async-start | bytes 3538944 | tf_op jit(solution)/shard_map/psum | solution.py:129
  430.3 17.5 %copy-start.77 = (bf16[1,4,1,64,512]{4,3,1,2,0:T(8,128)(2,1)S(1)}, bf16[1,4,1,64,512]{4,3,1,2,0:T(8,128)(2,1)}, u32[]{:S(2)}) copy-start(bf16[1,4,1,64,512]{4,3,1,2,0:T(8,128)(2,1)} %copy.661) | copy-start | bytes 786436
  430.3 18.2 %copy-start.73 = (bf16[1,4,1,64,512]{4,3,1,2,0:T(8,128)(2,1)S(1)}, bf16[1,4,1,64,512]{4,3,1,2,0:T(8,128)(2,1)}, u32[]{:S(2)}) copy-start(bf16[1,4,1,64,512]{4,3,1,2,0:T(8,128)(2,1)} %copy.662) | copy-start | bytes 786436
  432.3 16.9 %copy-start.69 = (bf16[1,4,1,64,512]{4,3,1,2,0:T(8,128)(2,1)S(1)}, bf16[1,4,1,64,512]{4,3,1,2,0:T(8,128)(2,1)}, u32[]{:S(2)}) copy-start(bf16[1,4,1,64,512]{4,3,1,2,0:T(8,128)(2,1)} %copy.663) | copy-start | bytes 786436
  434.0 15.9 %copy-start.44 = (bf16[1,4,1,64,512]{4,3,1,2,0:T(8,128)(2,1)S(1)}, bf16[1,4,1,64,512]{4,3,1,2,0:T(8,128)(2,1)}, u32[]{:S(2)}) copy-start(bf16[1,4,1,64,512]{4,3,1,2,0:T(8,128)(2,1)} %copy.664) | copy-start | bytes 786436
  435.7 14.9 %copy-start.10 = (bf16[1,4,64,512]{3,2,1,0:T(8,128)(2,1)S(1)}, bf16[1,4,64,512]{3,2,1,0:T(8,128)(2,1)}, u32[]{:S(2)}) copy-start(bf16[1,4,64,512]{3,2,1,0:T(8,128)(2,1)} %copy-done.9) | copy-start | bytes 786436
  465.0 68.0 %copy-start.11 = (f32[1,4,64,512]{3,2,1,0:T(8,128)S(1)}, f32[1,4,64,512]{3,2,1,0:T(8,128)}, u32[]{:S(2)}) copy-start(f32[1,4,64,512]{3,2,1,0:T(8,128)} %get-tuple-element.290) | copy-start | bytes 1572868
  465.0 68.0 %copy-start.92 = (bf16[1728,64,1]{0,1,2:T(8,128)(2,1)S(1)}, bf16[1728,64,1]{0,1,2:T(8,128)(2,1)}, u32[]{:S(2)}) copy-start(bf16[1728,64,1]{0,1,2:T(8,128)(2,1)} %reshape.2870) | copy-start | bytes 663556
  (301 other events, 2741.1 us)
Sparse Core Ops, SparseCore 0:
  370.8 162.0 all-reduce.4
  535.4 68.3 all-reduce.6
